TPU v7x, 32 devices: a whole 2x2x4 slice. The times are simulated.
32 devices in a mesh: member: 8 (over y, x, core), tile: 4 (over z).
Axes of the slice: x: 2, y: 2, z: 4, core: 2. Of those that a mesh axis runs over, the one named last changes fastest.
Arguments:
- node_fine: int32 [8, 12], P('member'), may hold values from 0 to 8
- node_coarse: int32 [32, 12], P('member'), may hold values from 0 to 8
- weight_fine: int32 [8], P('member'), may hold values from -3 to 3
- weight_coarse: int32 [32], P('member'), may hold values from -3 to 3
- mode_x: float32 [12, 64], replicated, may hold values from -1 to 1
- mode_y: float32 [12, 512], replicated, may hold values from -1 to 1
- mode_z: float32 [12, 32], replicated, may hold values from -1 to 1
- source_fine: float32 [64, 32, 512], P('tile'), may hold values from -12 to 12
- source_coarse: float32 [32, 16, 256], P(None, None, 'tile'), may hold values from -6 to 6
Outputs:
- combined: float32 [32, 16, 256], P('member', None, 'tile')
All inputs are finite; a program needn't handle non-finite values.
Results may differ from a plain program's by a relative error of at most 0.00026.
Values sent between devices are 32-bit elements; how exact they have to be, the bound alone decides.
No kernel may reach another device: no remote copies, remote signals or barrier semaphores. Data moves between devices by JAX's collectives and lax.ppermute only.
A program may use at most 192 MiB of HBM per device.

v0:
```python
import math
import jax
import jax.numpy as jnp
from jax import lax
from jax.sharding import PartitionSpec as P

NODES = 9
SWEEPS = 3
CENTRE = 1.125
HALF_WIDTH = 0.875
SPREAD_RATIO = CENTRE / HALF_WIDTH


def extended(block, sides, width):
    for axis, dim in sides:
        count = lax.axis_size(axis)
        forward = [(i, i + 1) for i in range(count - 1)]
        backward = [(target, source) for source, target in forward]
        low = lax.ppermute(
            lax.slice_in_dim(block, block.shape[dim] - width, None, axis=dim), axis, forward
        )
        high = lax.ppermute(lax.slice_in_dim(block, 0, width, axis=dim), axis, backward)
        block = jnp.concatenate([low, block, high], axis=dim)
    return block


def sweep_factors(sweep_count):
    previous = 1.0 / SPREAD_RATIO
    factors = []
    for _ in range(sweep_count - 1):
        current = 1.0 / (2.0 * SPREAD_RATIO - previous)
        factors.append((current * previous, 2.0 * current / HALF_WIDTH))
        previous = current
    return factors


def shifted(tensor, spatial, along_dim, offset):
    for current in spatial:
        begin_at = offset if current == along_dim else 1
        tensor = lax.slice_in_dim(
            tensor, begin_at, tensor.shape[current] - 2 + begin_at, axis=current
        )
    return tensor


def diagonal_of(cond_pad, spatial):
    centre = shifted(cond_pad, spatial, -1, 1)
    running = jnp.zeros_like(centre)
    for along_dim in spatial:
        for offset in (0, 2):
            running = running + 0.5 * (centre + shifted(cond_pad, spatial, along_dim, offset))
    return running


def apply_op(field_pad, cond_pad, spatial):
    centre_k = shifted(cond_pad, spatial, -1, 1)
    centre_v = shifted(field_pad, spatial, -1, 1)
    running = jnp.zeros_like(centre_v * centre_k)
    for along_dim in spatial:
        for offset in (0, 2):
            coupling = 0.5 * (centre_k + shifted(cond_pad, spatial, along_dim, offset))
            running = running + coupling * (
                centre_v - shifted(field_pad, spatial, along_dim, offset)
            )
    return running


def node_values(node_index):
    return jnp.cos(math.pi * node_index.astype(jnp.float32) / (NODES - 1))


def pair_mean(modes):
    return 0.5 * (modes[:, 0::2] + modes[:, 1::2])


def log_field(values, along_x, along_z, along_y):
    weighted = (along_x.T * values)[:, None, :] * along_z.T[None, :, :]
    flattened = weighted.reshape(weighted.shape[0] * weighted.shape[1], weighted.shape[2])
    product = jnp.dot(flattened, along_y, precision=lax.Precision.HIGHEST)
    return product.reshape(weighted.shape[0], weighted.shape[1], along_y.shape[1])


def log_batch(values, along_x, along_z, along_y):
    weighted = (along_x.T[None, :, :] * values[:, None, :])[:, :, None, :] * along_z.T[
        None, None, :, :
    ]
    shape_in = weighted.shape
    flattened = weighted.reshape(shape_in[0] * shape_in[1] * shape_in[2], shape_in[3])
    product = jnp.dot(flattened, along_y, precision=lax.Precision.HIGHEST)
    return product.reshape(shape_in[0], shape_in[1], shape_in[2], along_y.shape[1])


def restrict(tensor):
    blocks = tensor.reshape(
        tensor.shape[0] // 2, 2, tensor.shape[1] // 2, 2, tensor.shape[2] // 2, 2
    )
    return blocks.sum(axis=(1, 3, 5)) * 0.125


def trim_dim(tensor, trim_depth, along_dim):
    return lax.slice_in_dim(
        tensor, trim_depth, tensor.shape[along_dim] - trim_depth, axis=along_dim
    )


def pad_other(tensor, halo_dim, spatial):
    widths = []
    for position in range(tensor.ndim):
        if position in spatial and position != halo_dim:
            widths.append((1, 1))
        else:
            widths.append((0, 0))
    return jnp.pad(tensor, widths)


def smooth_deep(source_ext, cond_pad, halo_dim, spatial, inside, reach_cells, factors):
    diagonal = diagonal_of(cond_pad, spatial)
    safe_diag = diagonal + (1.0 - inside)
    update = source_ext / (CENTRE * safe_diag) * inside
    result = trim_dim(update, reach_cells, halo_dim)
    residual = source_ext
    extent = reach_cells
    for keep_part, push_part in factors:
        cond_part = trim_dim(cond_pad, reach_cells + 1 - extent, halo_dim)
        applied = apply_op(pad_other(update, halo_dim, spatial), cond_part, spatial)
        residual = trim_dim(residual, 1, halo_dim) - applied
        extent = extent - 1
        trim_depth = reach_cells - extent
        fresh = keep_part * trim_dim(update, 1, halo_dim) + push_part * residual / trim_dim(
            safe_diag, trim_depth, halo_dim
        )
        update = fresh * trim_dim(inside, trim_depth, halo_dim)
        result = result + trim_dim(update, extent, halo_dim)
    return result


def body(
    node_fine,
    node_coarse,
    weight_fine,
    weight_coarse,
    mode_x,
    mode_y,
    mode_z,
    source_fine,
    source_coarse,
):
    factors = sweep_factors(SWEEPS)
    reach_cells = SWEEPS - 1
    tile_place = lax.axis_index("tile")
    strip_width = source_fine.shape[0]
    coarse_width = source_coarse.shape[2]
    mode_xc = pair_mean(mode_x)
    mode_yc = pair_mean(mode_y)
    mode_zc = pair_mean(mode_z)
    extent = reach_cells + 1
    padded_x = jnp.pad(mode_x, ((0, 0), (extent, extent)))
    mode_slab = lax.dynamic_slice_in_dim(
        padded_x, tile_place * strip_width, strip_width + 2 * extent, 1
    )
    global_x = (
        tile_place * strip_width - extent + jnp.arange(strip_width + 2 * extent, dtype=jnp.int32)
    )
    inside_x = ((global_x >= 0) & (global_x < mode_x.shape[1])).astype(jnp.float32)
    conduct = (
        jnp.exp(log_field(node_values(node_fine[0]), mode_slab, mode_z, mode_y))
        * inside_x[:, None, None]
    )
    cond_fine = pad_other(conduct, 0, (0, 1, 2))
    padded_y = jnp.pad(mode_yc, ((0, 0), (extent, extent)))
    mode_strip = lax.dynamic_slice_in_dim(
        padded_y, tile_place * coarse_width, coarse_width + 2 * extent, 1
    )
    global_y = (
        tile_place * coarse_width - extent + jnp.arange(coarse_width + 2 * extent, dtype=jnp.int32)
    )
    inside_y = ((global_y >= 0) & (global_y < mode_yc.shape[1])).astype(jnp.float32)
    conduct_c = (
        jnp.exp(log_batch(node_values(node_coarse), mode_xc, mode_zc, mode_strip)) * inside_y
    )
    cond_coarse = pad_other(conduct_c, 3, (1, 2, 3))
    fine_ext = extended(source_fine, (("tile", 0),), reach_cells)
    fine_inside = trim_dim(inside_x, 1, 0)[:, None, None]
    fine_result = smooth_deep(fine_ext, cond_fine, 0, (0, 1, 2), fine_inside, reach_cells, factors)
    coarse_ext = extended(source_coarse, (("tile", 2),), reach_cells)
    coarse_inside = trim_dim(inside_y, 1, 0)[None, None, None, :]
    coarse_result = smooth_deep(
        coarse_ext[None], cond_coarse, 3, (1, 2, 3), coarse_inside, reach_cells, factors
    )
    fine_part = weight_fine[0].astype(jnp.float32) * restrict(fine_result)
    arrived = lax.all_to_all(fine_part, "tile", split_axis=2, concat_axis=0, tiled=True)
    coarse_part = jnp.tensordot(
        weight_coarse.astype(jnp.float32), coarse_result, axes=1, precision=lax.Precision.HIGHEST
    )
    summed = arrived + coarse_part
    return lax.psum_scatter(summed, "member", scatter_dimension=0, tiled=True)


def solution(mesh):
    return jax.shard_map(
        body,
        mesh=mesh,
        in_specs=(
            P("member", None),
            P("member", None),
            P("member"),
            P("member"),
            P(),
            P(),
            P(),
            P("tile", None, None),
            P(None, None, "tile"),
        ),
        out_specs=P("member", None, "tile"),
        check_vma=False,
    )
```

profile of v0, /device:TPU:0, one launch (start us, length us, event | category | flops | bytes accessed | tf_op | source)
XLA Modules:
  0.0 194.3 jit_solution(10056728130827275311)
XLA Ops:
  6.5 1.7 fusion.159
  8.3 5.6 %collective-permute-start = (f32[2,32,512]{2,1,0:T(8,128)}, f32[2,32,512]{2,1,0:T(8,128)}, u32[]{:S(2)}, u32[]{:S(2)}) collective-permute-start(f32[2,32,512]{2,1,0:T(8,128)} %get-tuple-element.14), channel_id=1, source_target_pairs={{0,1},{1,2},{2,3},{4,5},{5,6},{6,7},{8,9},{9,10},{10,11},{12,13},{... | collective-permute-start | bytes 393224 | tf_op jit(solution)/shard_map/ppermute | solution.py:19
  13.9 1.3 collective-permute-start.1
  15.2 1.2 fusion.160
  16.3 4.6 %collective-permute-start.2 = (f32[32,16,2]{2,1,0:T(8,128)S(1)}, f32[32,16,2]{2,1,0:T(8,128)S(1)}, u32[]{:S(2)}, u32[]{:S(2)}) collective-permute-start(f32[32,16,2]{2,1,0:T(8,128)S(1)} %get-tuple-element.15), channel_id=1, source_target_pairs={{0,1},{1,2},{2,3},{4,5},{5,6},{6,7},{8,9},{9,10},{10,11},{12,13},{... | collective-permute-start | bytes 12296 | tf_op jit(solution)/shard_map/ppermute | solution.py:19
  20.9 1.3 collective-permute-start.3
  22.2 0.1 slice.637
  22.4 0.1 slice.638
  22.5 0.5 slice.641
  23.0 0.5 slice.642
  23.5 0.1 slice.639
  23.6 0.1 slice.640
  23.8 0.1 multiply_bitcast_fusion.2
  23.9 0.1 copy.29
  24.0 0.1 broadcast_subtract_fusion.1
  24.1 0.1 copy.34
  24.3 0.1 slice_bitcast_fusion.2
  24.3 1.7 fusion
  26.1 0.1 broadcast_multiply_fusion.1
  26.2 1.9 fusion.1
  29.0 1.0 collective-permute-done.3
  30.0 0.2 pad_maximum_fusion
  30.2 0.1 copy.33
  30.3 0.2 fusion.161
  30.5 0.1 slice_bitcast_fusion
  30.7 0.1 copy.35
  30.8 1.7 divide_multiply_fusion.1
  32.5 4.2 %fusion.128 = (f32[4,32,16,66]{3,1,2,0:T(8,128)S(1)}, f32[4,32,16,66]{3,1,2,0:T(8,128)S(1)}) fusion(f32[4,32,16,68]{3,1,2,0:T(8,128)S(1)} %get-tuple-element.12, f32[4,32,16,68]{3,1,2,0:T(8,128)S(1)} %get-tuple-element.11, f32[66]{0:T(128)S(1)} %slice_bitcast_fusion.2, f32[4,32,16,70]{3,1,2,0:T(8,128)S(1)} %fusion.1, f32[32,16,66]{2,0,1:T(8,128)S(1)} %copy.35), kind=kLoop, calls=%fused_computation.183 | loop fusion | flops 4730880 | bytes 10781184 | tf_op jit(solution)/shard_map/mul | solution.py:132
  36.7 4.5 %fusion.133 = f32[4,32,16,64]{3,1,2,0:T(8,128)S(1)} fusion(f32[4,32,16,68]{3,1,2,0:T(8,128)S(1)} %get-tuple-element.11, f32[4,32,16,68]{3,1,2,0:T(8,128)S(1)} %get-tuple-element.12, f32[4,32,16,66]{3,1,2,0:T(8,128)S(1)} %get-tuple-element.9, f32[4,32,16,70]{3,1,2,0:T(8,128)S(1)} %fusion.1, f32[4,32,16,66]{3,1,2,0:T(8,128)S(1)} %get-tuple-element.10, ...), kind=kLoop, calls=%fused_computation.193 | loop fusion | flops 4849664 | bytes 12059136 | tf_op jit(solution)/shard_map/add | solution.py:133
  41.2 0.9 constant_dynamic-update-slice_fusion.2
  42.2 0.1 constant_dynamic-update-slice_fusion.1
  42.3 0.9 constant_dynamic-update-slice_fusion
  43.2 1.2 divide_multiply_fusion
  44.4 2.9 %fusion.35 = (f32[18,32,512]{2,1,0:T(8,128)S(1)}, f32[18,32,512]{2,1,0:T(8,128)S(1)}) fusion(f32[20,32,512]{2,1,0:T(8,128)S(1)} %get-tuple-element.8, f32[20,32,512]{2,1,0:T(8,128)S(1)} %get-tuple-element.7, f32[18]{0:T(128)S(1)} %slice.617, f32[22,32,512]{2,1,0:T(8,128)S(1)} %fusion, f32[20,32,512]{2,1,0:T(8,128)S(1)} %constant_dynamic-update-slice_fusion), kind=kLoop, calls=%fused_computation.81 | loop fusion | flops 10321920 | bytes 14549504 | tf_op jit(solution)/shard_map/mul | solution.py:132
  47.3 2.7 %fusion.139 = f32[16,32,512]{2,1,0:T(8,128)S(1)} fusion(f32[20,32,512]{2,1,0:T(8,128)S(1)} %get-tuple-element.7, f32[20,32,512]{2,1,0:T(8,128)S(1)} %get-tuple-element.8, f32[18,32,512]{2,1,0:T(8,128)S(1)} %get-tuple-element.5, f32[22,32,512]{2,1,0:T(8,128)S(1)} %fusion, f32[18,32,512]{2,1,0:T(8,128)S(1)} %get-tuple-element.6, f32[16]{0:T(128)S(1)} %slice.634), kind=kLoop, calls=%fused_computation.206 | loop fusion | flops 9699328 | bytes 13107712 | tf_op jit(solution)/shard_map/add | solution.py:133
  50.0 68.4 %reshape.50 = f32[8,2,16,2,256,2]{5,4,3,2,1,0:T(8,128)} reshape(f32[16,32,512]{2,1,0:T(8,128)S(1)} %fusion.139) | data formatting | bytes 2097152 | tf_op jit(solution)/shard_map/reshape | solution.py:94
  118.4 20.8 %reduce_sum.9 = f32[8,16,256]{2,1,0:T(8,128)S(1)} reduce(f32[8,2,16,2,256,2]{5,4,3,2,1,0:T(8,128)} %reshape.50, f32[]{:T(128)} %constant.18.clone.1), dimensions={1,3,5}, to_apply=%region_0.1 | reduce | flops 229376 | bytes 1179652 | tf_op jit(solution)/shard_map/reduce_sum | solution.py:97
  139.2 0.4 copy.30
  139.6 1.0 reshape.55
  140.7 4.9 %all-to-all-start = ((f32[4,1,8192]{2,1,0:T(1,128)}), f32[4,1,8192]{2,1,0:T(1,128)S(1)}, u32[]{:S(2)}, u32[]{:S(2)}) async-start(f32[4,1,8192]{2,1,0:T(1,128)} %reshape.55), calls=%async_computation | async-start | bytes 262144 | tf_op jit(solution)/shard_map/all_to_all | solution.py:191
  145.6 2.6 %fusion.140 = f32[1,32,16,64]{3,0,2,1:T(1,128)S(1)} fusion(f32[4,32,16,64]{3,1,2,0:T(8,128)S(1)} %fusion.133, s32[4]{0:T(128)S(1)} %copy-done.6), kind=kOutput, calls=%fused_computation.207 | convolution fusion | flops 1572868 | bytes 655376 | tf_op jit(solution)/shard_map/dot_general | solution.py:192
  148.1 3.3 %all-to-all-done = f32[4,1,8192]{2,1,0:T(1,128)S(1)} async-done(((f32[4,1,8192]{2,1,0:T(1,128)}), f32[4,1,8192]{2,1,0:T(1,128)S(1)}, u32[]{:S(2)}, u32[]{:S(2)}) %all-to-all-start) | async-done | bytes 131104 | tf_op jit(solution)/shard_map/all_to_all | solution.py:191
  151.5 0.5 broadcast.125
  152.0 1.0 reduce
  153.0 0.4 reshape.56
  153.4 0.4 copy.40
  153.8 0.7 bitcast_add_fusion
  154.6 32.9 %reduce-scatter.2.cloned.1.call-done = f32[4,16,64]{2,1,0:T(8,128)} async-done(((f32[32,16,64]{2,1,0:T(8,128)}), f32[4,16,64]{2,1,0:T(8,128)}) %reduce-scatter.2.cloned.1.call-update) | async-done | bytes 16400 | tf_op jit(solution)/shard_map/reduce_scatter | solution.py:196
  (34 shorter events, 0.5 us)
Async XLA Ops:
  6.5 15.7 %copy-start.4 = (f32[12,64]{1,0:T(8,128)S(1)}, f32[12,64]{1,0:T(8,128)}, u32[]{:S(2)}) copy-start(f32[12,64]{1,0:T(8,128)} %param.13) | copy-start | bytes 9220
  6.5 16.0 %copy-start.2 = (f32[12,512]{1,0:T(8,128)S(1)}, f32[12,512]{1,0:T(8,128)}, u32[]{:S(2)}) copy-start(f32[12,512]{1,0:T(8,128)} %param.14) | copy-start | bytes 73732
  6.5 17.0 %copy-start.3 = (f32[12,32]{1,0:T(8,128)S(1)}, f32[12,32]{1,0:T(8,128)}, u32[]{:S(2)}) copy-start(f32[12,32]{1,0:T(8,128)} %param.15) | copy-start | bytes 4612
  6.5 17.2 %copy-start.7 = (s32[1,12]{1,0:T(1,128)S(1)}, s32[1,12]{1,0:T(1,128)}, u32[]{:S(2)}) copy-start(s32[1,12]{1,0:T(1,128)} %param.9) | copy-start | bytes 148
  6.5 17.5 %copy-start.5 = (s32[4,12]{1,0:T(4,128)S(1)}, s32[4,12]{1,0:T(4,128)}, u32[]{:S(2)}) copy-start(s32[4,12]{1,0:T(4,128)} %param.10) | copy-start | bytes 580
  8.3 32.9 %collective-permute-start = (f32[2,32,512]{2,1,0:T(8,128)}, f32[2,32,512]{2,1,0:T(8,128)}, u32[]{:S(2)}, u32[]{:S(2)}) collective-permute-start(f32[2,32,512]{2,1,0:T(8,128)} %get-tuple-element.14), channel_id=1, source_target_pairs={{0,1},{1,2},{2,3},{4,5},{5,6},{6,7},{8,9},{9,10},{10,11},{12,13},{... | collective-permute-start | bytes 393224 | tf_op jit(solution)/shard_map/ppermute | solution.py:19
  13.9 28.4 %collective-permute-start.1 = (f32[2,32,512]{2,1,0:T(8,128)}, f32[2,32,512]{2,1,0:T(8,128)}, u32[]{:S(2)}, u32[]{:S(2)}) collective-permute-start(f32[2,32,512]{2,1,0:T(8,128)} %get-tuple-element.13), channel_id=1, source_target_pairs={{1,0},{2,1},{3,2},{5,4},{6,5},{7,6},{9,8},{10,9},{11,10},{13,12},{... | collective-permute-start | bytes 393224 | tf_op jit(solution)/shard_map/ppermute | solution.py:22
  16.3 12.6 %collective-permute-start.2 = (f32[32,16,2]{2,1,0:T(8,128)S(1)}, f32[32,16,2]{2,1,0:T(8,128)S(1)}, u32[]{:S(2)}, u32[]{:S(2)}) collective-permute-start(f32[32,16,2]{2,1,0:T(8,128)S(1)} %get-tuple-element.15), channel_id=1, source_target_pairs={{0,1},{1,2},{2,3},{4,5},{5,6},{6,7},{8,9},{9,10},{10,11},{12,13},{... | collective-permute-start | bytes 12296 | tf_op jit(solution)/shard_map/ppermute | solution.py:19
  20.9 9.1 %collective-permute-start.3 = (f32[32,16,2]{2,1,0:T(8,128)S(1)}, f32[32,16,2]{2,1,0:T(8,128)S(1)}, u32[]{:S(2)}, u32[]{:S(2)}) collective-permute-start(f32[32,16,2]{2,1,0:T(8,128)S(1)} %get-tuple-element.16), channel_id=1, source_target_pairs={{1,0},{2,1},{3,2},{5,4},{6,5},{7,6},{9,8},{10,9},{11,10},{13,12},{... | collective-permute-start | bytes 12296 | tf_op jit(solution)/shard_map/ppermute | solution.py:22
  24.3 5.7 %copy-start = (f32[32,16,64]{2,1,0:T(8,128)S(1)}, f32[32,16,64]{2,1,0:T(8,128)}, u32[]{:S(2)}) copy-start(f32[32,16,64]{2,1,0:T(8,128)} %param.17) | copy-start | bytes 393220
  36.7 5.5 %copy-start.1 = (f32[16,32,512]{2,1,0:T(8,128)S(1)}, f32[16,32,512]{2,1,0:T(8,128)}, u32[]{:S(2)}) copy-start(f32[16,32,512]{2,1,0:T(8,128)} %param.16) | copy-start | bytes 3145732
  139.2 6.4 %copy-start.6 = (s32[4]{0:T(128)S(1)}, s32[4]{0:T(128)}, u32[]{:S(2)}) copy-start(s32[4]{0:T(128)} %param.12) | copy-start | bytes 52
  140.7 10.8 %all-to-all-start = ((f32[4,1,8192]{2,1,0:T(1,128)}), f32[4,1,8192]{2,1,0:T(1,128)S(1)}, u32[]{:S(2)}, u32[]{:S(2)}) async-start(f32[4,1,8192]{2,1,0:T(1,128)} %reshape.55), calls=%async_computation | async-start | bytes 262144 | tf_op jit(solution)/shard_map/all_to_all | solution.py:191
  145.6 41.9 %reduce-scatter.2.cloned.1.call-start = ((), (), s32[]{:S(2)}) async-start(), calls=%async_computation.2 | async-start | bytes 294912 | tf_op jit(solution)/shard_map/reduce_scatter | solution.py:196
Sparse Core Ops, SparseCore 0:
  154.7 32.7 reduce-scatter.1
where the time goes:
time: 195 us; the launch traced here: 194 us
  local copies, waits for them, and re-layouts  78.2 us (40%)
  other arithmetic  40.5 us (21%)
  waiting for transfers between devices  37.3 us (19%)
  starting transfers between devices  17.7 us (9%)
  between operations  14.4 us (7%)
  matrix products  6.21 us (3%)
    reshape x1, local copies, waits for them, and re-layouts, restrict(): tensor.reshape(tensor.shape[0] // 2, 2, tensor.shape[1] // 2, 2, tensor.s...  68.4 us
    reduce_scatter x1, waiting for transfers between devices, body(): return lax.psum_scatter(summed, 'member', scatter_dimension=0, tiled=True)  32.9 us
    reduce_sum x1, other arithmetic, restrict(): return blocks.sum(axis=(1, 3, 5)) * 0.125  20.8 us
    ppermute x2, starting transfers between devices, extended(): lax.ppermute(lax.slice_in_dim(block, block.shape[dim] - width, None, axis...  10.2 us
    add x2, other arithmetic, smooth_deep(): result = result + trim_dim(update, extent, halo_dim)  7.19 us
    mul x2, other arithmetic, smooth_deep(): update = fresh * trim_dim(inside, trim_depth, halo_dim)  7.12 us
    all_to_all x1, starting transfers between devices, body(): lax.all_to_all(fine_part, 'tile', split_axis=2, concat_axis=0, tiled=True)  4.92 us
  transfers between devices with their start and end apart: 6, of which 3 were waited for; matrix products, arithmetic and copies ran while one was open for 11% of the time, Pallas kernels for 0%

commit v1 on v0

--- a/solution.py
+++ b/solution.py
@@ -188,7 +188,12 @@
         coarse_ext[None], cond_coarse, 3, (1, 2, 3), coarse_inside, reach_cells, factors
     )
     fine_part = weight_fine[0].astype(jnp.float32) * restrict(fine_result)
-    arrived = lax.all_to_all(fine_part, "tile", split_axis=2, concat_axis=0, tiled=True)
+    arrived = jnp.concatenate(
+        lax.all_to_all(
+            jnp.stack(jnp.split(fine_part, lax.axis_size("tile"), axis=2)), "tile", 0, 0
+        ),
+        axis=0,
+    )
     coarse_part = jnp.tensordot(
         weight_coarse.astype(jnp.float32), coarse_result, axes=1, precision=lax.Precision.HIGHEST
     )

time: 195 us -> 194 us (level)
  no operation moved by 1% of the time
where the time goes in v1:
time: 194 us; the launch traced here: 193 us
  local copies, waits for them, and re-layouts  77 us (40%)
  other arithmetic  40.6 us (21%)
  waiting for transfers between devices  37.3 us (19%)
  starting transfers between devices  17.7 us (9%)
  between operations  14.4 us (7%)
  matrix products  6.2 us (3%)
    reshape x1, local copies, waits for them, and re-layouts, restrict(): tensor.reshape(tensor.shape[0] // 2, 2, tensor.shape[1] // 2, 2, tensor.s...  68.4 us
    reduce_scatter x1, waiting for transfers between devices, body(): return lax.psum_scatter(summed, 'member', scatter_dimension=0, tiled=True)  32.9 us
    reduce_sum x1, other arithmetic, restrict(): return blocks.sum(axis=(1, 3, 5)) * 0.125  20.8 us
    ppermute x2, starting transfers between devices, extended(): lax.ppermute(lax.slice_in_dim(block, block.shape[dim] - width, None, axis...  10.2 us
    add x2, other arithmetic, smooth_deep(): result = result + trim_dim(update, extent, halo_dim)  7.19 us
    mul x2, other arithmetic, smooth_deep(): update = fresh * trim_dim(inside, trim_depth, halo_dim)  7.12 us
    all_to_all x1, starting transfers between devices, body(): lax.all_to_all(jnp.stack(jnp.split(fine_part, lax.axis_size('tile'), axis...  4.93 us
  transfers between devices with their start and end apart: 6, of which 3 were waited for; matrix products, arithmetic and copies ran while one was open for 11% of the time, Pallas kernels for 0%

profile of v1, /device:TPU:0, one launch (start us, length us, event | category | flops | bytes accessed | tf_op | source)
XLA Modules:
  0.0 193.2 jit_solution(6014242047671876361)
XLA Ops:
  6.5 1.7 fusion.159
  8.3 5.6 %collective-permute-start = (f32[2,32,512]{2,1,0:T(8,128)}, f32[2,32,512]{2,1,0:T(8,128)}, u32[]{:S(2)}, u32[]{:S(2)}) collective-permute-start(f32[2,32,512]{2,1,0:T(8,128)} %get-tuple-element.14), channel_id=1, source_target_pairs={{0,1},{1,2},{2,3},{4,5},{5,6},{6,7},{8,9},{9,10},{10,11},{12,13},{... | collective-permute-start | bytes 393224 | tf_op jit(solution)/shard_map/ppermute | solution.py:19
  13.9 1.3 collective-permute-start.1
  15.2 1.2 fusion.160
  16.3 4.6 %collective-permute-start.2 = (f32[32,16,2]{2,1,0:T(8,128)S(1)}, f32[32,16,2]{2,1,0:T(8,128)S(1)}, u32[]{:S(2)}, u32[]{:S(2)}) collective-permute-start(f32[32,16,2]{2,1,0:T(8,128)S(1)} %get-tuple-element.15), channel_id=1, source_target_pairs={{0,1},{1,2},{2,3},{4,5},{5,6},{6,7},{8,9},{9,10},{10,11},{12,13},{... | collective-permute-start | bytes 12296 | tf_op jit(solution)/shard_map/ppermute | solution.py:19
  20.9 1.3 collective-permute-start.3
  22.2 0.1 slice.637
  22.4 0.1 slice.638
  22.5 0.5 slice.641
  23.0 0.5 slice.642
  23.5 0.1 slice.639
  23.6 0.1 slice.640
  23.8 0.1 multiply_bitcast_fusion.2
  23.8 0.1 copy.14
  23.9 0.1 broadcast_subtract_fusion.1
  24.1 0.1 copy.16
  24.2 0.1 slice_bitcast_fusion.7
  24.2 0.1 slice_bitcast_fusion.6
  24.3 1.7 fusion
  26.1 0.1 broadcast_multiply_fusion.1
  26.1 1.9 %fusion.1 = f32[4,32,16,70]{3,1,2,0:T(8,128)S(1)} fusion(f32[70]{0:T(128)S(1)} %and_convert_fusion, f32[16,12]{1,0:T(8,128)S(1)} %copy.16, f32[4,32,12]{1,2,0:T(8,128)S(1)} %broadcast_multiply_fusion.1, s32[]{:T(128)S(6)} %select_n.7, f32[12,256]{1,0:T(8,128)S(1)} %add_multiply_fusion), kind=kOutput, calls=%fused_computation.43 | convolution fusion | flops 20811776 | bytes 592924 | tf_op jit(solution)/shard_map/dot_general | solution.py:89
  29.0 1.0 collective-permute-done.3
  30.0 0.2 pad_maximum_fusion.1
  30.2 0.1 copy.15
  30.3 0.2 fusion.161
  30.5 0.1 slice_bitcast_fusion
  30.7 0.1 copy.17
  30.7 1.7 divide_multiply_fusion.1
  32.4 4.2 %fusion.128 = (f32[4,32,16,66]{3,1,2,0:T(8,128)S(1)}, f32[4,32,16,66]{3,1,2,0:T(8,128)S(1)}) fusion(f32[4,32,16,68]{3,1,2,0:T(8,128)S(1)} %get-tuple-element.12, f32[4,32,16,68]{3,1,2,0:T(8,128)S(1)} %get-tuple-element.11, f32[66]{0:T(128)S(1)} %slice_bitcast_fusion.6, f32[4,32,16,70]{3,1,2,0:T(8,128)S(1)} %fusion.1, f32[32,16,66]{2,0,1:T(8,128)S(1)} %copy.17), kind=kLoop, calls=%fused_computation.183 | loop fusion | flops 4730880 | bytes 10781184 | tf_op jit(solution)/shard_map/mul | solution.py:132
  36.7 4.5 %fusion.133 = f32[4,32,16,64]{3,1,2,0:T(8,128)S(1)} fusion(f32[4,32,16,68]{3,1,2,0:T(8,128)S(1)} %get-tuple-element.11, f32[4,32,16,68]{3,1,2,0:T(8,128)S(1)} %get-tuple-element.12, f32[4,32,16,66]{3,1,2,0:T(8,128)S(1)} %get-tuple-element.9, f32[4,32,16,70]{3,1,2,0:T(8,128)S(1)} %fusion.1, f32[4,32,16,66]{3,1,2,0:T(8,128)S(1)} %get-tuple-element.10, ...), kind=kLoop, calls=%fused_computation.193 | loop fusion | flops 4849664 | bytes 12059136 | tf_op jit(solution)/shard_map/add | solution.py:133
  41.2 0.9 constant_dynamic-update-slice_fusion.2
  42.2 0.1 constant_dynamic-update-slice_fusion.1
  42.3 0.9 constant_dynamic-update-slice_fusion
  43.2 1.2 divide_multiply_fusion
  44.4 2.9 %fusion.35 = (f32[18,32,512]{2,1,0:T(8,128)S(1)}, f32[18,32,512]{2,1,0:T(8,128)S(1)}) fusion(f32[20,32,512]{2,1,0:T(8,128)S(1)} %get-tuple-element.8, f32[20,32,512]{2,1,0:T(8,128)S(1)} %get-tuple-element.7, f32[18]{0:T(128)S(1)} %slice.617, f32[22,32,512]{2,1,0:T(8,128)S(1)} %fusion, f32[20,32,512]{2,1,0:T(8,128)S(1)} %constant_dynamic-update-slice_fusion), kind=kLoop, calls=%fused_computation.81 | loop fusion | flops 10321920 | bytes 14549504 | tf_op jit(solution)/shard_map/mul | solution.py:132
  47.3 2.7 %fusion.139 = f32[16,32,512]{2,1,0:T(8,128)S(1)} fusion(f32[20,32,512]{2,1,0:T(8,128)S(1)} %get-tuple-element.7, f32[20,32,512]{2,1,0:T(8,128)S(1)} %get-tuple-element.8, f32[18,32,512]{2,1,0:T(8,128)S(1)} %get-tuple-element.5, f32[22,32,512]{2,1,0:T(8,128)S(1)} %fusion, f32[18,32,512]{2,1,0:T(8,128)S(1)} %get-tuple-element.6, f32[16]{0:T(128)S(1)} %slice.634), kind=kLoop, calls=%fused_computation.206 | loop fusion | flops 9699328 | bytes 13107712 | tf_op jit(solution)/shard_map/add | solution.py:133
  50.0 68.4 %reshape.53 = f32[8,2,16,2,256,2]{5,4,3,2,1,0:T(8,128)} reshape(f32[16,32,512]{2,1,0:T(8,128)S(1)} %fusion.139) | data formatting | bytes 2097152 | tf_op jit(solution)/shard_map/reshape | solution.py:94
  118.4 20.8 %reduce_sum.9 = f32[8,16,256]{2,1,0:T(8,128)S(1)} reduce(f32[8,2,16,2,256,2]{5,4,3,2,1,0:T(8,128)} %reshape.53, f32[]{:T(128)} %constant.18.clone.1), dimensions={1,3,5}, to_apply=%region_0.1 | reduce | flops 229376 | bytes 1179652 | tf_op jit(solution)/shard_map/reduce_sum | solution.py:97
  139.2 0.1 slice_bitcast_fusion.4
  139.3 0.8 reshape.59
  140.2 4.9 %all-to-all-start = ((f32[4,1,8192]{2,1,0:T(1,128)}), f32[4,1,8192]{2,1,0:T(1,128)S(1)}, u32[]{:S(2)}, u32[]{:S(2)}) async-start(f32[4,1,8192]{2,1,0:T(1,128)} %reshape.59), calls=%async_computation | async-start | bytes 262144 | tf_op jit(solution)/shard_map/all_to_all | solution.py:192
  145.1 2.6 %fusion.140 = f32[1,32,16,64]{3,0,2,1:T(1,128)S(1)} fusion(f32[4,32,16,64]{3,1,2,0:T(8,128)S(1)} %fusion.133, s32[4]{0:T(128)S(1)} %copy-done.6), kind=kOutput, calls=%fused_computation.207 | convolution fusion | flops 1572868 | bytes 655376 | tf_op jit(solution)/shard_map/dot_general | solution.py:197
  147.7 3.4 %all-to-all-done = f32[4,1,8192]{2,1,0:T(1,128)S(1)} async-done(((f32[4,1,8192]{2,1,0:T(1,128)}), f32[4,1,8192]{2,1,0:T(1,128)S(1)}, u32[]{:S(2)}, u32[]{:S(2)}) %all-to-all-start) | async-done | bytes 131104 | tf_op jit(solution)/shard_map/all_to_all | solution.py:192
  151.0 0.5 broadcast.125
  151.5 1.0 reduce
  152.5 0.2 reshape.60
  152.7 0.7 bitcast_add_fusion
  153.4 32.9 %reduce-scatter.2.cloned.1.call-done = f32[4,16,64]{2,1,0:T(8,128)} async-done(((f32[32,16,64]{2,1,0:T(8,128)}), f32[4,16,64]{2,1,0:T(8,128)}) %reduce-scatter.2.cloned.1.call-update) | async-done | bytes 16400 | tf_op jit(solution)/shard_map/reduce_scatter | solution.py:201
  (33 shorter events, 0.4 us)
Async XLA Ops:
  6.5 15.7 %copy-start.4 = (f32[12,64]{1,0:T(8,128)S(1)}, f32[12,64]{1,0:T(8,128)}, u32[]{:S(2)}) copy-start(f32[12,64]{1,0:T(8,128)} %param.13) | copy-start | bytes 9220
  6.5 16.0 %copy-start.2 = (f32[12,512]{1,0:T(8,128)S(1)}, f32[12,512]{1,0:T(8,128)}, u32[]{:S(2)}) copy-start(f32[12,512]{1,0:T(8,128)} %param.14) | copy-start | bytes 73732
  6.5 16.9 %copy-start.3 = (f32[12,32]{1,0:T(8,128)S(1)}, f32[12,32]{1,0:T(8,128)}, u32[]{:S(2)}) copy-start(f32[12,32]{1,0:T(8,128)} %param.15) | copy-start | bytes 4612
  6.5 17.2 %copy-start.7 = (s32[1,12]{1,0:T(1,128)S(1)}, s32[1,12]{1,0:T(1,128)}, u32[]{:S(2)}) copy-start(s32[1,12]{1,0:T(1,128)} %param.9) | copy-start | bytes 148
  6.5 17.5 %copy-start.5 = (s32[4,12]{1,0:T(4,128)S(1)}, s32[4,12]{1,0:T(4,128)}, u32[]{:S(2)}) copy-start(s32[4,12]{1,0:T(4,128)} %param.10) | copy-start | bytes 580
  8.3 32.9 %collective-permute-start = (f32[2,32,512]{2,1,0:T(8,128)}, f32[2,32,512]{2,1,0:T(8,128)}, u32[]{:S(2)}, u32[]{:S(2)}) collective-permute-start(f32[2,32,512]{2,1,0:T(8,128)} %get-tuple-element.14), channel_id=1, source_target_pairs={{0,1},{1,2},{2,3},{4,5},{5,6},{6,7},{8,9},{9,10},{10,11},{12,13},{... | collective-permute-start | bytes 393224 | tf_op jit(solution)/shard_map/ppermute | solution.py:19
  13.9 28.4 %collective-permute-start.1 = (f32[2,32,512]{2,1,0:T(8,128)}, f32[2,32,512]{2,1,0:T(8,128)}, u32[]{:S(2)}, u32[]{:S(2)}) collective-permute-start(f32[2,32,512]{2,1,0:T(8,128)} %get-tuple-element.13), channel_id=1, source_target_pairs={{1,0},{2,1},{3,2},{5,4},{6,5},{7,6},{9,8},{10,9},{11,10},{13,12},{... | collective-permute-start | bytes 393224 | tf_op jit(solution)/shard_map/ppermute | solution.py:22
  16.3 12.6 %collective-permute-start.2 = (f32[32,16,2]{2,1,0:T(8,128)S(1)}, f32[32,16,2]{2,1,0:T(8,128)S(1)}, u32[]{:S(2)}, u32[]{:S(2)}) collective-permute-start(f32[32,16,2]{2,1,0:T(8,128)S(1)} %get-tuple-element.15), channel_id=1, source_target_pairs={{0,1},{1,2},{2,3},{4,5},{5,6},{6,7},{8,9},{9,10},{10,11},{12,13},{... | collective-permute-start | bytes 12296 | tf_op jit(solution)/shard_map/ppermute | solution.py:19
  20.9 9.1 %collective-permute-start.3 = (f32[32,16,2]{2,1,0:T(8,128)S(1)}, f32[32,16,2]{2,1,0:T(8,128)S(1)}, u32[]{:S(2)}, u32[]{:S(2)}) collective-permute-start(f32[32,16,2]{2,1,0:T(8,128)S(1)} %get-tuple-element.16), channel_id=1, source_target_pairs={{1,0},{2,1},{3,2},{5,4},{6,5},{7,6},{9,8},{10,9},{11,10},{13,12},{... | collective-permute-start | bytes 12296 | tf_op jit(solution)/shard_map/ppermute | solution.py:22
  24.3 5.7 %copy-start = (f32[32,16,64]{2,1,0:T(8,128)S(1)}, f32[32,16,64]{2,1,0:T(8,128)}, u32[]{:S(2)}) copy-start(f32[32,16,64]{2,1,0:T(8,128)} %param.17) | copy-start | bytes 393220
  36.7 5.5 %copy-start.1 = (f32[16,32,512]{2,1,0:T(8,128)S(1)}, f32[16,32,512]{2,1,0:T(8,128)}, u32[]{:S(2)}) copy-start(f32[16,32,512]{2,1,0:T(8,128)} %param.16) | copy-start | bytes 3145732
  139.2 5.9 %copy-start.6 = (s32[4]{0:T(128)S(1)}, s32[4]{0:T(128)}, u32[]{:S(2)}) copy-start(s32[4]{0:T(128)} %param.12) | copy-start | bytes 52
  140.2 10.9 %all-to-all-start = ((f32[4,1,8192]{2,1,0:T(1,128)}), f32[4,1,8192]{2,1,0:T(1,128)S(1)}, u32[]{:S(2)}, u32[]{:S(2)}) async-start(f32[4,1,8192]{2,1,0:T(1,128)} %reshape.59), calls=%async_computation | async-start | bytes 262144 | tf_op jit(solution)/shard_map/all_to_all | solution.py:192
  145.1 41.2 %reduce-scatter.2.cloned.1.call-start = ((), (), s32[]{:S(2)}) async-start(), calls=%async_computation.2 | async-start | bytes 294912 | tf_op jit(solution)/shard_map/reduce_scatter | solution.py:201
Sparse Core Ops, SparseCore 0:
  153.5 32.7 reduce-scatter.1
